TPU v7x, 512 devices: a whole 4x8x8 slice. The times are simulated.
512 devices in a mesh: tm: 16 (over y, core), sta: 32 (over z, x).
Axes of the slice: x: 4, y: 8, z: 8, core: 2. Of those that a mesh axis runs over, the one named last changes fastest.
Arguments:
- spectra: bfloat16 [16, 2048, 2048], P('tm', 'sta'), may hold values from -5 to 5
- pair_list: int32 [16, 32, 256], P('tm', 'sta'), may hold values from 0 to 511, as said below
- pair_stations: int32 [2, 16384], P(None, 'sta'), may hold values from 0 to 2047
- owner_code: int32 [16384], P('sta'), may hold values from 0 to 1023, as said below
Outputs:
- stack: float32 [32768, 1024], P(('tm', 'sta'))
Inputs may be any that keep to these rules, and one draw needn't show every extreme that they name: `pair_list`: within each (g, s) the entries are distinct catalogue numbers below 512. `owner_code`: within each catalogue of 512 pairs the codes are distinct; each owner (code // 64) holds at most 64 pairs of a catalogue, and in every catalogue one owner holds exactly 64.
All inputs are finite; a program needn't handle non-finite values.
Results may differ from a plain program's by a relative error of at most 0.0003.
Values may be sent and summed in bfloat16 or wider, within the bound.
A program may use at most 64 MiB of HBM per device.

v0:
```python
import jax
import jax.numpy as jnp
from jax import lax
from jax.sharding import PartitionSpec as P

LAGS = 1024


def lag_table(bins, lags):
    bin_index = jnp.arange(bins, dtype=jnp.int32)[:, None]
    lag_index = jnp.arange(lags, dtype=jnp.int32)[None, :] - lags // 2
    phase = (bin_index * lag_index % (2 * bins)).astype(jnp.float32) * (jnp.pi / bins)
    scale = 1.0 / bins**0.5
    return jnp.concatenate([jnp.cos(phase) * scale, -jnp.sin(phase) * scale], axis=0)


def cross_spectra(first, second, bins):
    first = first.astype(jnp.float32)
    second = second.astype(jnp.float32)
    real_a, imag_a = (first[..., :bins], first[..., bins:])
    real_b, imag_b = (second[..., :bins], second[..., bins:])
    real_c = real_a * real_b + imag_a * imag_b
    imag_c = real_a * imag_b - imag_a * real_b
    return jnp.concatenate([real_c, imag_c], axis=-1)


def local(spectra, pair_list, pair_stations, owner_code):
    local_spectra = spectra[0]
    width = local_spectra.shape[1]
    bins = width // 2
    catalogue = pair_stations.shape[1]
    groups = lax.axis_size("tm")
    capacity = 2 * catalogue // groups
    listed = pair_list[0, 0]
    first_station = pair_stations[0][listed]
    second_station = pair_stations[1][listed]
    codes = owner_code[listed]
    table = lag_table(bins, LAGS)
    all_spectra = lax.all_gather(local_spectra, "sta", axis=0, tiled=True)
    first = all_spectra[first_station]
    second = all_spectra[second_station]
    cross = cross_spectra(first, second, bins)
    partial_lags = jnp.dot(
        cross, table, precision=lax.Precision.HIGHEST, preferred_element_type=jnp.float32
    )
    slots = jnp.arange(capacity * lax.axis_size("tm"), dtype=jnp.int32)
    select = (slots[:, None] == codes[None, :]).astype(jnp.float32)
    return lax.psum_scatter(
        jnp.dot(
            select,
            partial_lags,
            precision=lax.Precision.HIGHEST,
            preferred_element_type=jnp.float32,
        ),
        "tm",
        scatter_dimension=0,
        tiled=True,
    )


def solution(mesh):
    return jax.shard_map(
        local,
        mesh=mesh,
        in_specs=(P("tm", "sta", None), P("tm", "sta", None), P(None, "sta"), P("sta")),
        out_specs=P(("tm", "sta"), None),
        check_vma=False,
    )
```

profile of v0, /device:TPU:1, one launch (start us, length us, event | category | flops | bytes accessed | tf_op | source)
XLA Modules:
  0.0 216.2 jit_solution(13112215413817106566)
XLA Ops:
  6.5 0.0 copy-start
  6.5 0.0 all-gather.3.cloned.1.call-start
  6.5 0.7 all-gather.3.cloned.1.call-update
  7.3 0.0 reduce-scatter.2.cloned.1.call-start
  7.3 0.7 compare_select_fusion.2
  8.0 0.0 copy-done
  8.0 1.9 gather_fusion
  10.0 0.8 fusion.16
  10.7 1.9 gather_fusion.1
  12.7 1.9 gather_fusion.3
  14.7 18.2 %cosine_multiply_fusion = (f32[1024,1024]{1,0:T(8,128)}, f32[1024,1024]{1,0:T(8,128)}) fusion(s32[1024]{0:T(1024)S(1)} %iota_add_fusion), kind=kLoop, calls=%fused_computation.16 | loop fusion | flops 17825792 | bytes 8392704 | tf_op jit(solution)/shard_map/mul | solution.py:14
  32.9 86.5 %all-gather.3.cloned.1.call-done = bf16[1,2048,2048]{2,1,0:T(8,128)(2,1)} async-done(((bf16[1,64,2048]{2,1,0:T(8,128)(2,1)}), bf16[1,2048,2048]{2,1,0:T(8,128)(2,1)}) %all-gather.3.cloned.1.call-update) | async-done | bytes 8388624 | tf_op jit(solution)/shard_map/all_gather | solution.py:39
  119.4 6.8 %gather_fusion.2 = bf16[256,2048]{1,0:T(8,128)(2,1)S(1)} fusion(bf16[2048,2048]{1,0:T(8,128)(2,1)} %bitcast.13, s32[1024]{0:T(1024)S(1)} %pad_clamp_fusion.1), kind=kCustom, calls=%fused_computation.2 | custom fusion | bytes 2098176 | tf_op jit(solution)/shard_map/gather | solution.py:40
  126.2 6.8 %gather_fusion.4 = bf16[256,2048]{1,0:T(8,128)(2,1)S(1)} fusion(bf16[2048,2048]{1,0:T(8,128)(2,1)} %bitcast.14, s32[1024]{0:T(1024)S(1)} %pad_clamp_fusion), kind=kCustom, calls=%fused_computation.4 | custom fusion | bytes 2098176 | tf_op jit(solution)/shard_map/gather | solution.py:41
  133.0 0.2 convert_element_type.13
  133.3 0.0 copy-start.1
  133.3 0.0 copy-start.2
  133.3 0.2 convert_element_type.12
  133.5 0.6 multiply_add_fusion
  134.2 1.3 copy-done.1
  135.5 1.3 copy-done.2
  136.7 7.5 %fusion = f32[256,1024]{1,0:T(8,128)S(1)} fusion(f32[1024,1024]{1,0:T(8,128)S(1)} %copy-done.2, f32[1024,1024]{1,0:T(8,128)S(1)} %copy-done.1, f32[256,1024]{1,0:T(8,128)S(1)} %get-tuple-element.6, f32[256,1024]{1,0:T(8,128)S(1)} %get-tuple-element.5), kind=kOutput, calls=%fused_computation.5 | convolution fusion | flops 6445072384 | bytes 11534336 | tf_op jit(solution)/shard_map/dot_general | solution.py:43
  144.3 3.8 %fusion.13 = f32[1024,1024]{1,0:T(8,128)} fusion(f32[256,1024]{1,0:T(8,128)S(1)} %fusion, s32[256]{0:T(256)S(1)} %gather_fusion), kind=kOutput, calls=%fused_computation.26 | convolution fusion | flops 3221487616 | bytes 5243904 | tf_op jit(solution)/shard_map/dot_general | solution.py:49
  148.1 0.0 reduce-scatter.2.cloned.1.call-update
  148.1 61.2 %reduce-scatter.2.cloned.1.call-done = f32[64,1024]{1,0:T(8,128)} async-done(((f32[1024,1024]{1,0:T(8,128)}), f32[64,1024]{1,0:T(8,128)}) %reduce-scatter.2.cloned.1.call-update) | async-done | bytes 262160 | tf_op jit(solution)/shard_map/reduce_scatter | solution.py:48
  (6 shorter events, 0.0 us)
Async XLA Ops:
  6.5 1.5 copy-start
  6.5 112.8 %all-gather.3.cloned.1.call-start = ((), (), s32[]{:S(2)}) async-start(), calls=%async_computation.2 | async-start | bytes 8650752 | tf_op jit(solution)/shard_map/all_gather | solution.py:39
  7.3 202.1 %reduce-scatter.2.cloned.1.call-start = ((), (), s32[]{:S(2)}) async-start(), calls=%async_computation.1 | async-start | bytes 4456448 | tf_op jit(solution)/shard_map/reduce_scatter | solution.py:48
  133.3 2.2 %copy-start.1 = (f32[1024,1024]{1,0:T(8,128)S(1)}, f32[1024,1024]{1,0:T(8,128)}, u32[]{:S(2)}) copy-start(f32[1024,1024]{1,0:T(8,128)} %get-tuple-element.9) | copy-start | bytes 12582916
  133.3 3.5 %copy-start.2 = (f32[1024,1024]{1,0:T(8,128)S(1)}, f32[1024,1024]{1,0:T(8,128)}, u32[]{:S(2)}) copy-start(f32[1024,1024]{1,0:T(8,128)} %get-tuple-element.10) | copy-start | bytes 12582916
Sparse Core Ops, SparseCore 0:
  10.5 108.8 all-gather.2
  148.3 61.0 reduce-scatter.1
where the time goes:
time: 218 us; the launch traced here: 216 us
  waiting for transfers between devices  148 us (68%)
  local copies, waits for them, and re-layouts  22.8 us (10%)
  other arithmetic  20 us (9%)
  between operations  13.5 us (6%)
  matrix products  11.4 us (5%)
    all_gather x1, waiting for transfers between devices, local(): all_spectra = lax.all_gather(local_spectra, 'sta', axis=0, tiled=True)  86.5 us
    reduce_scatter x1, waiting for transfers between devices, local(): lax.psum_scatter(jnp.dot(select, partial_lags, precision=lax.Precision.HI...  61.2 us
    mul x1, other arithmetic, lag_table(): jnp.cos(phase) * scale  18.2 us
    dot_general x1, matrix products, local(): jnp.dot(cross, table, precision=lax.Precision.HIGHEST, preferred_element_...  7.55 us
    gather x1, local copies, waits for them, and re-layouts, local(): second = all_spectra[second_station]  6.83 us
    gather x1, local copies, waits for them, and re-layouts, local(): first = all_spectra[first_station]  6.83 us
  transfers between devices with their start and end apart: 2, of which 2 were waited for; matrix products, arithmetic and copies ran while one was open for 12% of the time, Pallas kernels for 0%

commit v1 on v0

v1 whole, which is shorter than its diff:
```python
import functools

import jax
import jax.numpy as jnp
from jax import lax
from jax.experimental import pallas as pl
from jax.experimental.pallas import tpu as pltpu
from jax.sharding import PartitionSpec as P

LAGS = 1024
NX, NZ, NY = 4, 8, 8
MESH = pl.DeviceIdType.MESH


def place(axis):
    sta = lax.axis_index("sta")
    tm = lax.axis_index("tm")
    x, z = lax.rem(sta, NX), lax.div(sta, NX)
    y, core = lax.div(tm, 2), lax.rem(tm, 2)
    if axis == "z":
        return z, NZ, lambda j: {"sta": j * NX + x}
    if axis == "x":
        return x, NX, lambda j: {"sta": z * NX + j}
    if axis == "tm":
        return tm, 2 * NY, lambda j: {"tm": j}
    if axis == "y":
        return y, NY, lambda j: {"tm": j * 2 + core}
    return core, 2, lambda j: {"tm": y * 2 + j}


def exchange_kernel(axis, modes, *refs):
    count = len(modes)
    ins, outs = refs[:count], refs[count : 2 * count]
    send_sem, recv_sem, own_sem = refs[2 * count :]
    me, size, peer = place(axis)
    barrier = pltpu.get_barrier_semaphore()
    for k in range(1, size):
        pl.semaphore_signal(
            barrier, inc=1, device_id=peer(lax.rem(me + k, size)), device_id_type=MESH
        )
    owns = []
    for i, mode in enumerate(modes):
        own = pltpu.make_async_copy(
            ins[i].at[me] if mode == "swap" else ins[i], outs[i].at[me], own_sem.at[i]
        )
        own.start()
        owns.append(own)
    pl.semaphore_wait(barrier, size - 1)
    sends = []
    for k in range(1, size):
        to = lax.rem(me + k, size)
        for i, mode in enumerate(modes):
            copy = pltpu.make_async_remote_copy(
                src_ref=ins[i].at[to] if mode == "swap" else ins[i],
                dst_ref=outs[i].at[me],
                send_sem=send_sem.at[i, k],
                recv_sem=recv_sem.at[i, k],
                device_id=peer(to),
                device_id_type=MESH,
            )
            copy.start()
            sends.append((copy, i, k))
    for copy, i, k in sends:
        copy.wait_send()
    for copy, i, k in sends:
        origin = lax.rem(me + size - k, size)
        pltpu.make_async_remote_copy(
            src_ref=outs[i].at[origin],
            dst_ref=outs[i].at[origin],
            send_sem=send_sem.at[i, k],
            recv_sem=recv_sem.at[i, k],
            device_id=peer(origin),
            device_id_type=MESH,
        ).wait_recv()
    for own in owns:
        own.wait()


def exchange(axis, identity, *pairs):
    size = {"z": NZ, "x": NX, "tm": 2 * NY, "y": NY, "core": 2}[axis]
    modes = tuple(mode for mode, _ in pairs)
    arrays = [array for _, array in pairs]
    shapes = [
        jax.ShapeDtypeStruct(
            array.shape if mode == "swap" else (size,) + array.shape, array.dtype
        )
        for mode, array in pairs
    ]
    count = len(pairs)
    vmem = pl.BlockSpec(memory_space=pltpu.VMEM)
    return pl.pallas_call(
        functools.partial(exchange_kernel, axis, modes),
        out_shape=shapes,
        in_specs=[vmem] * count,
        out_specs=[vmem] * count,
        scratch_shapes=[
            pltpu.SemaphoreType.DMA((count, size)),
            pltpu.SemaphoreType.DMA((count, size)),
            pltpu.SemaphoreType.DMA((count,)),
        ],
        compiler_params=pltpu.CompilerParams(
            collective_id=identity, has_side_effects=True
        ),
        name=f"exchange_{axis}",
    )(*arrays)


def stack_kernel(index_ref, mask_ref, data_ref, out_ref):
    first = index_ref[0, 0:1, :]
    second = index_ref[0, 1:2, :]
    code = index_ref[0, 2:3, :]
    pairs = first.shape[1]
    block = data_ref.shape[2]

    def pick(rows):
        total = None
        for part in range(data_ref.shape[0]):
            lane = lax.broadcasted_iota(jnp.int32, (block, pairs), 0) + part * block
            chosen = jnp.where(lane == rows, 1.0, 0.0).astype(jnp.bfloat16)
            term = jnp.dot(data_ref[part], chosen, preferred_element_type=jnp.float32)
            total = term if total is None else total + term
        return total.reshape(total.shape[0] // 16, 2, 8, pairs)

    a = pick(first)
    b = pick(second)
    mask = mask_ref[0].astype(jnp.float32)[:, None, :]
    real = jnp.sum((a[:, 0] * b[:, 0] + a[:, 1] * b[:, 1]) * mask, axis=0)
    imag = jnp.sum((a[:, 0] * b[:, 1] - a[:, 1] * b[:, 0]) * mask, axis=0)
    value = jnp.concatenate([real, imag], axis=0)
    high = value.astype(jnp.bfloat16)
    low = (value - high.astype(jnp.float32)).astype(jnp.bfloat16)
    slots = out_ref.shape[2]
    slot = lax.broadcasted_iota(jnp.int32, (slots, pairs), 0)
    chosen = jnp.where(slot == code, 1.0, 0.0).astype(jnp.bfloat16)
    contract = (((1,), (1,)), ((), ()))
    out_ref[0] = lax.dot_general(
        high, chosen, contract, preferred_element_type=jnp.float32
    ) + lax.dot_general(low, chosen, contract, preferred_element_type=jnp.float32)


def angles(bins, scale_bins):
    lag = jnp.arange(LAGS, dtype=jnp.int32)[None, :] - LAGS // 2
    phase = (bins[:, None] * lag) % (2 * scale_bins)
    phase = phase.astype(jnp.float32) * (jnp.pi / scale_bins)
    return jnp.cos(phase), jnp.sin(phase)


def half_table(bins):
    core = lax.axis_index("tm") % 2
    coarse = jnp.arange(NZ, dtype=jnp.int32) * (bins // NZ)
    number = jnp.arange(NY * 8, dtype=jnp.int32)
    fine = (number // 8 * 2 + core) * 8 + number % 8
    cos_c, sin_c = angles(coarse, bins)
    cos_f, sin_f = angles(fine, bins)
    scale = 1.0 / bins**0.5
    cos_c, sin_c = (cos_c * scale)[None, :, None], (sin_c * scale)[None, :, None]
    cos_f, sin_f = cos_f.reshape(NY, 1, 8, LAGS), sin_f.reshape(NY, 1, 8, LAGS)
    real = cos_c * cos_f - sin_c * sin_f
    imag = -(sin_c * cos_f + cos_c * sin_f)
    return jnp.stack([real, imag], axis=2).reshape(bins, LAGS)


def local(spectra, pair_list, pair_stations, owner_code):
    stations, width = spectra.shape[1:]
    bins = width // 2
    catalogue = owner_code.shape[0]
    groups = 2 * NY
    slots = 2 * catalogue
    f = bins // (NZ * groups)
    table = half_table(bins)
    shard, inner = pair_stations // stations, pair_stations % stations
    column = (shard % NX) * (NZ * stations) + (shard // NX) * stations + inner
    number = jnp.arange(catalogue, dtype=jnp.int32)
    listed = jnp.any(number[:, None] == pair_list[0, 0][None, :], axis=1)
    index = jnp.concatenate(
        [
            column,
            owner_code[None],
            listed.astype(jnp.int32)[None],
            jnp.zeros((4, catalogue), jnp.int32),
        ]
    )
    blocks = spectra[0].reshape(stations, 2, NZ, bins // NZ).transpose(2, 0, 1, 3)
    blocks = blocks.reshape(NZ, stations, 2 * bins // NZ)
    blocks, index = exchange("z", 0, ("swap", blocks), ("copy", index))
    mask = index[:, 3, :].astype(jnp.bfloat16).reshape(16, NZ * catalogue // 16)
    turned = blocks.reshape(NZ * stations, 2, groups, f).transpose(2, 1, 3, 0)
    turned = turned.reshape(groups, 2 * f, NZ * stations)
    turned, mask = exchange("tm", 1, ("swap", turned), ("copy", mask))
    (data,) = exchange("x", 2, ("copy", turned.reshape(groups * 2 * f, NZ * stations)))
    mask = mask.reshape(groups, NZ, catalogue).transpose(1, 0, 2)
    stacked = pl.pallas_call(
        stack_kernel,
        grid=(NZ,),
        out_shape=jax.ShapeDtypeStruct((NZ, 2 * f, slots), jnp.float32),
        in_specs=[
            pl.BlockSpec((1, 8, catalogue), lambda c: (c, 0, 0)),
            pl.BlockSpec((1, groups, catalogue), lambda c: (c, 0, 0)),
            pl.BlockSpec(data.shape, lambda c: (0, 0, 0)),
        ],
        out_specs=pl.BlockSpec((1, 2 * f, slots), lambda c: (c, 0, 0)),
        name="stack_pairs",
    )(index, mask, data)
    (stacked,) = exchange("z", 3, ("swap", stacked))
    stacked = stacked.reshape(NZ * 2 * f, NY, slots // NY).transpose(1, 0, 2)
    (stacked,) = exchange("y", 4, ("swap", stacked))
    halves = lax.dot_general(
        stacked.reshape(bins, slots // NY),
        table,
        (((0,), (0,)), ((), ())),
        precision=lax.Precision.HIGHEST,
        preferred_element_type=jnp.float32,
    )
    (halves,) = exchange("core", 5, ("swap", halves.reshape(2, slots // groups, LAGS)))
    return halves[0] + halves[1]


def solution(mesh):
    return jax.shard_map(
        local,
        mesh=mesh,
        in_specs=(P("tm", "sta", None), P("tm", "sta", None), P(None, "sta"), P("sta")),
        out_specs=P(("tm", "sta"), None),
        check_vma=False,
    )
```

time: 218 us -> 144 us (0.66)
  waiting for transfers between devices: 148 us -> 0 us
  Pallas kernels: 0 us -> 121 us
  local copies, waits for them, and re-layouts: 22.8 us -> 9.06 us
  between operations: 13.5 us -> 0.18 us
  other arithmetic: 20 us -> 7.77 us
  matrix products: 11.4 us -> 5.39 us
    pallas_call x0 -> x7, Pallas kernels: none -> 121 us  [the longest x6 104 us: exchange(): pl.pallas_call(functools.partial(exchange_kernel, axis, modes), out_shape...]
    all_gather x1 -> x0, waiting for transfers between devices: 86.5 us -> none  [local(): all_spectra = lax.all_gather(local_spectra, 'sta', axis=0, tiled=True)]
    reduce_scatter x1 -> x0, waiting for transfers between devices: 61.2 us -> none  [local(): lax.psum_scatter(jnp.dot(select, partial_lags, precision=lax.Precision.HI...]
    gather x5 -> x0, local copies, waits for them, and re-layouts: 19.5 us -> none  [the longest x1 6.83 us: local(): second = all_spectra[second_station]]
    mul x1 -> x2, other arithmetic: 18.2 us -> 0.22 us  [the longest x1 0.21 us: half_table(): cos_c * scale]
    dot_general x2 -> x1, matrix products: 11.4 us -> 5.39 us  [local(): lax.dot_general(stacked.reshape(bins, slots // NY), table, (((0,), (0,)),...]
    reshape x0 -> x6, local copies, waits for them, and re-layouts: none -> 4.47 us  [the longest x2 1.65 us: local(): mask = mask.reshape(groups, NZ, catalogue).transpose(1, 0, 2)]
    another operation x0 -> x1, other arithmetic: none -> 2.25 us  [half_table(): return jnp.stack([real, imag], axis=2).reshape(bins, LAGS)]
  transfers between devices with their start and end apart: 2 -> 0, of which waited for: 2 -> 0; matrix products, arithmetic and copies ran while one was open for 12% -> 0% of each run, Pallas kernels for 0% -> 0%
where the time goes in v1:
time: 144 us; the launch traced here: 143 us
  Pallas kernels  121 us (84%)
  local copies, waits for them, and re-layouts  9.06 us (6%)
  other arithmetic  7.77 us (5%)
  matrix products  5.39 us (4%)
    pallas_call x6, Pallas kernels, exchange(): pl.pallas_call(functools.partial(exchange_kernel, axis, modes), out_shape...  104 us
    pallas_call x1, Pallas kernels, local(): pl.pallas_call(stack_kernel, grid=(NZ,), out_shape=jax.ShapeDtypeStruct((...  17.3 us
    dot_general x1, matrix products, local(): lax.dot_general(stacked.reshape(bins, slots // NY), table, (((0,), (0,)),...  5.39 us

profile of v1, /device:TPU:1, one launch (start us, length us, event | category | flops | bytes accessed | tf_op | source)
XLA Modules:
  0.0 143.4 jit_solution(6663672066996653187)
XLA Ops:
  0.0 1.1 fusion.5
  1.1 0.2 cosine_multiply_fusion
  1.4 0.6 multiply_subtract_fusion
  2.0 0.0 copy-start
  2.0 0.0 copy-start.1
  2.0 0.0 copy-start.3
  2.0 0.0 copy-start.2
  2.0 2.3 %pad_maximum_fusion = f32[8,8,2,8,1024]{4,3,2,1,0:T(8,128)} fusion(f32[8,8,1,8,1024]{4,3,2,1,0:T(8,128)S(1)} %get-tuple-element.14, f32[8,8,1,8,1024]{4,3,2,1,0:T(8,128)S(1)} %get-tuple-element.13), kind=kLoop, calls=%fused_computation | loop fusion | flops 1048576 | bytes 8388608 | tf_op jit(solution)/shard_map/stack | solution.py:160
  4.2 0.0 copy-done
  4.3 0.2 copy.27
  4.5 0.9 reshape.207.refs_0_
  5.4 0.0 copy-done.1
  5.4 0.0 copy-done.3
  5.4 0.2 fusion
  5.6 0.1 pad.5.clone
  5.7 0.0 copy-done.2
  5.7 0.7 add_add_fusion.refs_1_
  6.4 21.1 %exchange_z.2 = (bf16[8,64,256]{2,1,0:T(8,128)(2,1)}, s32[8,8,512]{2,1,0:T(8,128)}) custom-call(bf16[8,64,256]{2,1,0:T(8,128)(2,1)} %reshape.207.refs_0_, s32[8,512]{1,0:T(8,128)} %add_add_fusion.refs_1_), custom_call_target="tpu_custom_call" | custom-call | tf_op jit(solution)/shard_map/exchange_z/pallas_call | solution.py:91
  27.4 1.0 fusion.9
  28.4 0.6 convert_element_type.46.refs_1_
  29.0 1.3 copy.15
  30.3 0.3 reshape.208
  30.6 0.7 copy_bitcast_fusion.1.refs_0_
  31.3 20.8 %exchange_tm.1 = (bf16[16,16,512]{2,1,0:T(8,128)(2,1)}, bf16[16,16,256]{2,1,0:T(8,128)(2,1)}) custom-call(bf16[16,16,512]{2,1,0:T(8,128)(2,1)} %copy_bitcast_fusion.1.refs_0_, bf16[16,256]{1,0:T(8,128)(2,1)} %convert_element_type.46.refs_1_), custom_call_target="tpu_custom_call" | custom-call | tf_op jit(solution)/shard_map/exchange_tm/pallas_call | solution.py:91
  52.1 18.0 %exchange_x.1.data_ref = bf16[4,256,512]{2,1,0:T(8,128)(2,1)} custom-call(bf16[256,512]{1,0:T(8,128)(2,1)} %bitcast.47), custom_call_target="tpu_custom_call" | custom-call | tf_op jit(solution)/shard_map/exchange_x/pallas_call | solution.py:91
  70.1 1.0 reshape.210
  71.1 0.7 copy.28
  71.8 17.3 %stack_pairs.1.refs_0_ = f32[8,16,1024]{2,1,0:T(8,128)} custom-call(s32[8,8,512]{2,1,0:T(8,128)} %get-tuple-element.9.index_ref, bf16[8,16,512]{2,1,0:T(8,128)(2,1)} %bitcast.46, bf16[4,256,512]{2,1,0:T(8,128)(2,1)} %exchange_x.1.data_ref), custom_call_target="tpu_custom_call" | custom-call | tf_op jit(solution)/shard_map/stack_pairs/pallas_call | solution.py:192
  89.1 19.5 %exchange_z.3 = f32[8,16,1024]{2,1,0:T(8,128)} custom-call(f32[8,16,1024]{2,1,0:T(8,128)} %stack_pairs.1.refs_0_), custom_call_target="tpu_custom_call" | custom-call | tf_op jit(solution)/shard_map/exchange_z/pallas_call | solution.py:91
  108.6 1.1 copy.21
  109.7 0.9 copy.26
  110.6 18.8 %exchange_y.1 = f32[8,128,128]{2,1,0:T(8,128)} custom-call(f32[8,128,128]{2,1,0:T(8,128)} %bitcast.42), custom_call_target="tpu_custom_call" | custom-call | tf_op jit(solution)/shard_map/exchange_y/pallas_call | solution.py:91
  129.4 1.2 copy.19
  130.7 5.4 %fusion.22.refs_0_ = f32[2,64,1024]{2,1,0:T(8,128)} fusion(f32[2,64,1024]{2,1,0:T(8,128)S(1)} %bitcast.39, f32[1024,1024,1]{1,0,2:T(8,128)} %bitcast.38), kind=kOutput, calls=%fused_computation.61 | convolution fusion | flops 1610612736 | bytes 5242880 | tf_op jit(solution)/shard_map/dot_general | solution.py:207
  136.1 5.6 %exchange_core.1 = f32[2,64,1024]{2,1,0:T(8,128)} custom-call(f32[2,64,1024]{2,1,0:T(8,128)} %fusion.22.refs_0_), custom_call_target="tpu_custom_call" | custom-call | tf_op jit(solution)/shard_map/exchange_core/pallas_call | solution.py:91
  141.6 1.8 %add_bitcast_fusion = f32[64,1024]{1,0:T(8,128)} fusion(f32[2,64,1024]{2,1,0:T(8,128)} %exchange_core.1), kind=kLoop, calls=%fused_computation.16 | loop fusion | flops 65536 | bytes 786432 | tf_op jit(solution)/shard_map/add | solution.py:215
  (7 shorter events, 0.1 us)
Async XLA Ops:
  2.0 2.3 %copy-start = (bf16[1,64,2048]{2,1,0:T(8,128)(2,1)S(1)}, bf16[1,64,2048]{2,1,0:T(8,128)(2,1)}, u32[]{:S(2)}) copy-start(bf16[1,64,2048]{2,1,0:T(8,128)(2,1)} %param.4) | copy-start | bytes 786436
  2.0 3.4 %copy-start.1 = (s32[2,512]{1,0:T(2,128)S(1)}, s32[2,512]{1,0:T(2,128)}, u32[]{:S(2)}) copy-start(s32[2,512]{1,0:T(2,128)} %param.6) | copy-start | bytes 12292
  2.0 3.4 %copy-start.3 = (s32[1,1,256]{2,1,0:T(1,128)S(1)}, s32[1,1,256]{2,1,0:T(1,128)}, u32[]{:S(2)}) copy-start(s32[1,1,256]{2,1,0:T(1,128)} %param.5) | copy-start | bytes 3076
  2.0 3.7 %copy-start.2 = (s32[512]{0:T(512)S(1)}, s32[512]{0:T(512)}, u32[]{:S(2)}) copy-start(s32[512]{0:T(512)} %param.7) | copy-start | bytes 6148

commit v2 on v1

--- a/solution.py
+++ b/solution.py
@@ -76,6 +76,108 @@
         own.wait()
 
 
+def greet(groups):
+    barrier = pltpu.get_barrier_semaphore()
+    for me, size, peer in groups:
+        for k in range(1, size):
+            pl.semaphore_signal(
+                barrier, inc=1, device_id=peer(lax.rem(me + k, size)), device_id_type=MESH
+            )
+    return barrier, sum(size - 1 for _, size, _ in groups)
+
+
+def remote(src, dst, send_sem, recv_sem, device):
+    return pltpu.make_async_remote_copy(
+        src_ref=src,
+        dst_ref=dst,
+        send_sem=send_sem,
+        recv_sem=recv_sem,
+        device_id=device,
+        device_id_type=MESH,
+    )
+
+
+def turn_kernel(
+    block_ref, mask_ref, data_ref, masks_ref,
+    t_send, t_recv, m_send, m_recv, x_send, x_recv, own_sem,
+):
+    me, size, peer = place("tm")
+    x, wide, beside = place("x")
+    barrier, count = greet([(me, size, peer), (x, wide, beside)])
+    own = pltpu.make_async_copy(block_ref.at[me], data_ref.at[x, me], own_sem.at[0])
+    own_mask = pltpu.make_async_copy(mask_ref, masks_ref.at[me], own_sem.at[1])
+    own.start()
+    own_mask.start()
+    pl.semaphore_wait(barrier, count)
+    order = sorted(range(1, size), key=lambda k: min(k, size - k))
+    pending = []
+
+    def forward(k, src, group):
+        for j in range(1, wide):
+            copy = remote(
+                src,
+                data_ref.at[x, group],
+                x_send.at[k, j],
+                x_recv.at[k, j],
+                beside(lax.rem(x + j, wide)),
+            )
+            copy.start()
+            pending.append(copy)
+
+    for k in order:
+        to = lax.rem(me + k, size)
+        copy = remote(
+            block_ref.at[to], data_ref.at[x, me], t_send.at[k], t_recv.at[k], peer(to)
+        )
+        copy.start()
+        pending.append(copy)
+    forward(0, block_ref.at[me], me)
+    for k in order:
+        to = lax.rem(me + k, size)
+        copy = remote(mask_ref, masks_ref.at[me], m_send.at[k], m_recv.at[k], peer(to))
+        copy.start()
+        pending.append(copy)
+    for k in order:
+        origin = lax.rem(me + size - k, size)
+        landed = data_ref.at[x, origin]
+        remote(landed, landed, t_send.at[k], t_recv.at[k], peer(origin)).wait_recv()
+        forward(k, landed, origin)
+    for k in order:
+        origin = lax.rem(me + size - k, size)
+        landed = masks_ref.at[origin]
+        remote(landed, landed, m_send.at[k], m_recv.at[k], peer(origin)).wait_recv()
+    for k in [0] + order:
+        group = lax.rem(me + size - k, size)
+        for j in range(1, wide):
+            origin = lax.rem(x + wide - j, wide)
+            landed = data_ref.at[origin, group]
+            remote(
+                landed, landed, x_send.at[k, j], x_recv.at[k, j], beside(origin)
+            ).wait_recv()
+    for copy in pending:
+        copy.wait_send()
+    own.wait()
+    own_mask.wait()
+
+
+def turn(blocks, mask):
+    size = 2 * NY
+    vmem = pl.BlockSpec(memory_space=pltpu.VMEM)
+    dma = pltpu.SemaphoreType.DMA
+    return pl.pallas_call(
+        turn_kernel,
+        out_shape=[
+            jax.ShapeDtypeStruct((NX,) + blocks.shape, blocks.dtype),
+            jax.ShapeDtypeStruct((size,) + mask.shape, mask.dtype),
+        ],
+        in_specs=[vmem] * 2,
+        out_specs=[vmem] * 2,
+        scratch_shapes=[dma((size,))] * 4 + [dma((size, NX))] * 2 + [dma((2,))],
+        compiler_params=pltpu.CompilerParams(collective_id=1, has_side_effects=True),
+        name="turn",
+    )(blocks, mask)
+
+
 def exchange(axis, identity, *pairs):
     size = {"z": NZ, "x": NX, "tm": 2 * NY, "y": NY, "core": 2}[axis]
     modes = tuple(mode for mode, _ in pairs)
@@ -105,10 +207,10 @@
     )(*arrays)
 
 
-def stack_kernel(index_ref, mask_ref, data_ref, out_ref):
-    first = index_ref[0, 0:1, :]
-    second = index_ref[0, 1:2, :]
-    code = index_ref[0, 2:3, :]
+def stack_one(index_ref, mask_ref, data_ref, result_ref, c):
+    first = index_ref[c, 0:1, :]
+    second = index_ref[c, 1:2, :]
+    code = index_ref[c, 2:3, :]
     pairs = first.shape[1]
     block = data_ref.shape[2]
 
@@ -123,19 +225,126 @@
 
     a = pick(first)
     b = pick(second)
-    mask = mask_ref[0].astype(jnp.float32)[:, None, :]
+    mask = mask_ref[c][:, None, :]
     real = jnp.sum((a[:, 0] * b[:, 0] + a[:, 1] * b[:, 1]) * mask, axis=0)
     imag = jnp.sum((a[:, 0] * b[:, 1] - a[:, 1] * b[:, 0]) * mask, axis=0)
     value = jnp.concatenate([real, imag], axis=0)
     high = value.astype(jnp.bfloat16)
     low = (value - high.astype(jnp.float32)).astype(jnp.bfloat16)
-    slots = out_ref.shape[2]
+    slots = result_ref.shape[2]
     slot = lax.broadcasted_iota(jnp.int32, (slots, pairs), 0)
     chosen = jnp.where(slot == code, 1.0, 0.0).astype(jnp.bfloat16)
     contract = (((1,), (1,)), ((), ()))
-    out_ref[0] = lax.dot_general(
+    result_ref[c] = lax.dot_general(
         high, chosen, contract, preferred_element_type=jnp.float32
     ) + lax.dot_general(low, chosen, contract, preferred_element_type=jnp.float32)
+
+
+def stack_kernel(
+    index_ref, mask_ref, data_ref, out_ref,
+    result_ref, landed_ref, z_send, z_recv, y_send, y_recv, own_sem,
+):
+    z, deep, along = place("z")
+    y, tall, above = place("y")
+    width = out_ref.shape[3]
+    barrier, count = greet([(z, deep, along), (y, tall, above)])
+
+    def compute(k):
+        stack_one(index_ref, mask_ref, data_ref, result_ref, lax.rem(z + k, deep))
+
+    def send(k):
+        to = lax.rem(z + k, deep)
+        return remote(
+            result_ref.at[to], landed_ref.at[z], z_send.at[k], z_recv.at[k], along(to)
+        )
+
+    def lanes(j):
+        return pl.ds(pl.multiple_of(j * width, width), width)
+
+    def share(k, origin, src_ref):
+        own = pltpu.make_async_copy(
+            src_ref.at[origin, :, lanes(y)], out_ref.at[y, origin], own_sem.at[k]
+        )
+        away = []
+        for j in range(1, tall):
+            to = lax.rem(y + j, tall)
+            away.append(
+                remote(
+                    src_ref.at[origin, :, lanes(to)],
+                    out_ref.at[y, origin],
+                    y_send.at[k, j],
+                    y_recv.at[k, j],
+                    above(to),
+                )
+            )
+        return own, away
+
+    def forward(k, origin, src_ref):
+        own, away = share(k, origin, src_ref)
+        own.start()
+        for copy in away:
+            copy.start()
+
+    def receive(k):
+        origin = lax.rem(z + deep - k, deep)
+        landed = landed_ref.at[origin]
+        remote(landed, landed, z_send.at[k], z_recv.at[k], along(origin)).wait_recv()
+        forward(k, origin, landed_ref)
+
+    compute(0)
+    pl.semaphore_wait(barrier, count)
+
+    @pl.loop(1, deep)
+    def _(k):
+        compute(k)
+
+        @pl.when(k == 1)
+        def _():
+            forward(0, z, result_ref)
+
+        @pl.when(k >= 2)
+        def _():
+            send(k - 1).start()
+
+        @pl.when(k >= 3)
+        def _():
+            receive(k - 2)
+
+    send(deep - 1).start()
+    receive(deep - 2)
+    receive(deep - 1)
+    for k in range(deep):
+        if k:
+            send(k).wait_send()
+        origin = lax.rem(z + deep - k, deep)
+        own, away = share(k, origin, landed_ref if k else result_ref)
+        own.wait()
+        for copy in away:
+            copy.wait_send()
+        for j in range(1, tall):
+            below = lax.rem(y + tall - j, tall)
+            arrived = out_ref.at[below, origin]
+            remote(
+                arrived, arrived, y_send.at[k, j], y_recv.at[k, j], above(below)
+            ).wait_recv()
+
+
+def stack_pairs(index, mask, data, slots):
+    rows = 16
+    vmem = pl.BlockSpec(memory_space=pltpu.VMEM)
+    dma = pltpu.SemaphoreType.DMA
+    return pl.pallas_call(
+        stack_kernel,
+        out_shape=jax.ShapeDtypeStruct((NY, NZ, rows, slots // NY), jnp.float32),
+        in_specs=[vmem] * 3,
+        out_specs=vmem,
+        scratch_shapes=[pltpu.VMEM((NZ, rows, slots), jnp.float32)] * 2
+        + [dma((NZ,))] * 2
+        + [dma((NZ, NY))] * 2
+        + [dma((NZ,))],
+        compiler_params=pltpu.CompilerParams(collective_id=2, has_side_effects=True),
+        name="stack_pairs",
+    )(index, mask, data)
 
 
 def angles(bins, scale_bins):
@@ -183,35 +392,20 @@
     blocks = spectra[0].reshape(stations, 2, NZ, bins // NZ).transpose(2, 0, 1, 3)
     blocks = blocks.reshape(NZ, stations, 2 * bins // NZ)
     blocks, index = exchange("z", 0, ("swap", blocks), ("copy", index))
-    mask = index[:, 3, :].astype(jnp.bfloat16).reshape(16, NZ * catalogue // 16)
+    mask = index[:, 3, :].astype(jnp.bfloat16)
     turned = blocks.reshape(NZ * stations, 2, groups, f).transpose(2, 1, 3, 0)
-    turned = turned.reshape(groups, 2 * f, NZ * stations)
-    turned, mask = exchange("tm", 1, ("swap", turned), ("copy", mask))
-    (data,) = exchange("x", 2, ("copy", turned.reshape(groups * 2 * f, NZ * stations)))
-    mask = mask.reshape(groups, NZ, catalogue).transpose(1, 0, 2)
-    stacked = pl.pallas_call(
-        stack_kernel,
-        grid=(NZ,),
-        out_shape=jax.ShapeDtypeStruct((NZ, 2 * f, slots), jnp.float32),
-        in_specs=[
-            pl.BlockSpec((1, 8, catalogue), lambda c: (c, 0, 0)),
-            pl.BlockSpec((1, groups, catalogue), lambda c: (c, 0, 0)),
-            pl.BlockSpec(data.shape, lambda c: (0, 0, 0)),
-        ],
-        out_specs=pl.BlockSpec((1, 2 * f, slots), lambda c: (c, 0, 0)),
-        name="stack_pairs",
-    )(index, mask, data)
-    (stacked,) = exchange("z", 3, ("swap", stacked))
-    stacked = stacked.reshape(NZ * 2 * f, NY, slots // NY).transpose(1, 0, 2)
-    (stacked,) = exchange("y", 4, ("swap", stacked))
+    data, mask = turn(turned.reshape(groups, 2 * f, NZ * stations), mask)
+    data = data.reshape(NX, groups * 2 * f, NZ * stations)
+    mask = mask.astype(jnp.float32).transpose(1, 0, 2)
+    stacked = stack_pairs(index, mask, data, slots)
     halves = lax.dot_general(
         stacked.reshape(bins, slots // NY),
         table,
         (((0,), (0,)), ((), ())),
-        precision=lax.Precision.HIGHEST,
+        precision=lax.Precision.HIGH,
         preferred_element_type=jnp.float32,
     )
-    (halves,) = exchange("core", 5, ("swap", halves.reshape(2, slots // groups, LAGS)))
+    (halves,) = exchange("core", 3, ("swap", halves.reshape(2, slots // groups, LAGS)))
     return halves[0] + halves[1]
 
 

time: 144 us -> 116 us (0.81)
  Pallas kernels: 121 us -> 96.7 us
  local copies, waits for them, and re-layouts: 9.06 us -> 5.75 us
    pallas_call x6 -> x2, Pallas kernels: 104 us -> 26.8 us  [exchange(): pl.pallas_call(functools.partial(exchange_kernel, axis, modes), out_shape...]
    pallas_call x1 -> x2, Pallas kernels: 17.3 us -> 69.9 us  [the longest x1 41.1 us: stack_pairs(): pl.pallas_call(stack_kernel, out_shape=jax.ShapeDtypeStruct((NY, NZ, rows...]
    reshape x4 -> x1, local copies, waits for them, and re-layouts: 3.28 us -> 0.73 us  [local(): data, mask = turn(turned.reshape(groups, 2 * f, NZ * stations), mask)]
    transpose x0 -> x1, other arithmetic: none -> 1.65 us  [local(): mask = mask.astype(jnp.float32).transpose(1, 0, 2)]
where the time goes in v2:
time: 116 us
  Pallas kernels  96.7 us (83%)
  other arithmetic  9.07 us (8%)
  local copies, waits for them, and re-layouts  5.75 us (5%)
  matrix products  4.34 us (4%)
    pallas_call x1, Pallas kernels, stack_pairs(): pl.pallas_call(stack_kernel, out_shape=jax.ShapeDtypeStruct((NY, NZ, rows...  41.1 us
    pallas_call x1, Pallas kernels, turn(): pl.pallas_call(turn_kernel, out_shape=[jax.ShapeDtypeStruct((NX,) + block...  28.8 us
    pallas_call x2, Pallas kernels, exchange(): pl.pallas_call(functools.partial(exchange_kernel, axis, modes), out_shape...  26.8 us
    dot_general x1, matrix products, local(): lax.dot_general(stacked.reshape(bins, slots // NY), table, (((0,), (0,)),...  4.34 us

profile of v2, /device:TPU:1, one launch (start us, length us, event | category | flops | bytes accessed | tf_op | source)
XLA Modules:
  0.0 116.0 jit_solution(18199383058232149608)
XLA Ops:
  0.0 1.1 fusion.5
  1.1 0.2 cosine_multiply_fusion
  1.4 0.6 multiply_subtract_fusion
  2.0 0.0 copy-start
  2.0 0.0 copy-start.1
  2.0 0.0 copy-start.3
  2.0 0.0 copy-start.2
  2.0 2.3 %pad_maximum_fusion = f32[8,8,2,8,1024]{4,3,2,1,0:T(8,128)} fusion(f32[8,8,1,8,1024]{4,3,2,1,0:T(8,128)S(1)} %get-tuple-element.14, f32[8,8,1,8,1024]{4,3,2,1,0:T(8,128)S(1)} %get-tuple-element.13), kind=kLoop, calls=%fused_computation | loop fusion | flops 1048576 | bytes 8388608 | tf_op jit(solution)/shard_map/stack | solution.py:369
  4.3 0.0 copy-done
  4.3 0.2 copy.26
  4.5 0.9 reshape.199.refs_0_
  5.4 0.0 copy-done.1
  5.4 0.0 copy-done.3
  5.4 0.2 fusion
  5.6 0.1 pad.5.clone
  5.7 0.0 copy-done.2
  5.7 0.7 add_add_fusion.refs_1_
  6.4 21.1 %exchange_z.1 = (bf16[8,64,256]{2,1,0:T(8,128)(2,1)}, s32[8,8,512]{2,1,0:T(8,128)}) custom-call(bf16[8,64,256]{2,1,0:T(8,128)(2,1)} %reshape.199.refs_0_, s32[8,512]{1,0:T(8,128)} %add_add_fusion.refs_1_), custom_call_target="tpu_custom_call" | custom-call | tf_op jit(solution)/shard_map/exchange_z/pallas_call | solution.py:193
  27.4 1.0 copy.19
  28.4 0.6 fusion.9.mask_ref
  29.0 1.3 %copy.17 = bf16[8,64,256]{1,0,2:T(8,128)(2,1)S(1)} copy(bf16[8,64,256]{2,1,0:T(8,128)(2,1)} %get-tuple-element.10) | data formatting | bytes 524288 | tf_op jit(solution)/shard_map/exchange_z/pallas_call | solution.py:193
  30.3 0.3 reshape.200
  30.6 0.7 copy_bitcast_fusion.block_ref
  31.4 28.8 %turn.1 = (bf16[4,16,16,512]{3,2,1,0:T(8,128)(2,1)}, bf16[16,8,512]{2,1,0:T(8,128)(2,1)}) custom-call(bf16[16,16,512]{2,1,0:T(8,128)(2,1)} %copy_bitcast_fusion.block_ref, bf16[8,512]{1,0:T(8,128)(2,1)} %fusion.9.mask_ref), custom_call_target="tpu_custom_call" | custom-call | tf_op jit(solution)/shard_map/turn/pallas_call | solution.py:167
  60.2 1.7 %convert_bitcast_fusion.mask_ref = f32[8,16,512]{2,1,0:T(8,128)} fusion(bf16[16,8,512]{2,1,0:T(8,128)(2,1)} %get-tuple-element.11), kind=kLoop, calls=%fused_computation.15 | loop fusion | flops 65536 | bytes 393216 | tf_op jit(solution)/shard_map/transpose | solution.py:399
  61.8 41.1 %stack_pairs.1 = f32[8,8,16,128]{3,2,1,0:T(8,128)} custom-call(s32[8,8,512]{2,1,0:T(8,128)} %get-tuple-element.9.index_ref, f32[8,16,512]{2,1,0:T(8,128)} %convert_bitcast_fusion.mask_ref, bf16[4,256,512]{2,1,0:T(8,128)(2,1)} %bitcast.38), custom_call_target="tpu_custom_call" | custom-call | tf_op jit(solution)/shard_map/stack_pairs/pallas_call | solution.py:336
  103.0 1.2 %copy.21 = f32[128,1024]{1,0:T(8,128)S(1)} copy(f32[128,1024]{0,1:T(8,128)} %bitcast.35) | data formatting | bytes 1048576 | tf_op jit(solution)/shard_map/dot_general | solution.py:401
  104.2 4.3 %fusion.22.refs_0_ = f32[2,64,1024]{2,1,0:T(8,128)} fusion(f32[2,64,1024]{2,1,0:T(8,128)S(1)} %bitcast.34, f32[1024,1024,1]{1,0,2:T(8,128)} %bitcast.33), kind=kOutput, calls=%fused_computation.60 | convolution fusion | flops 805306368 | bytes 5242880 | tf_op jit(solution)/shard_map/dot_general | solution.py:401
  108.6 5.7 %exchange_core.1 = f32[2,64,1024]{2,1,0:T(8,128)} custom-call(f32[2,64,1024]{2,1,0:T(8,128)} %fusion.22.refs_0_), custom_call_target="tpu_custom_call" | custom-call | tf_op jit(solution)/shard_map/exchange_core/pallas_call | solution.py:193
  114.3 1.8 %add_bitcast_fusion = f32[64,1024]{1,0:T(8,128)} fusion(f32[2,64,1024]{2,1,0:T(8,128)} %exchange_core.1), kind=kLoop, calls=%fused_computation.16 | loop fusion | flops 65536 | bytes 786432 | tf_op jit(solution)/shard_map/add | solution.py:409
  (7 shorter events, 0.1 us)
Async XLA Ops:
  2.0 2.3 %copy-start = (bf16[1,64,2048]{2,1,0:T(8,128)(2,1)S(1)}, bf16[1,64,2048]{2,1,0:T(8,128)(2,1)}, u32[]{:S(2)}) copy-start(bf16[1,64,2048]{2,1,0:T(8,128)(2,1)} %param.4) | copy-start | bytes 786436
  2.0 3.4 %copy-start.1 = (s32[2,512]{1,0:T(2,128)S(1)}, s32[2,512]{1,0:T(2,128)}, u32[]{:S(2)}) copy-start(s32[2,512]{1,0:T(2,128)} %param.6) | copy-start | bytes 12292
  2.0 3.5 %copy-start.3 = (s32[1,1,256]{2,1,0:T(1,128)S(1)}, s32[1,1,256]{2,1,0:T(1,128)}, u32[]{:S(2)}) copy-start(s32[1,1,256]{2,1,0:T(1,128)} %param.5) | copy-start | bytes 3076
  2.0 3.7 %copy-start.2 = (s32[512]{0:T(512)S(1)}, s32[512]{0:T(512)}, u32[]{:S(2)}) copy-start(s32[512]{0:T(512)} %param.7) | copy-start | bytes 6148

commit v3 on v2

--- a/solution.py
+++ b/solution.py
@@ -112,17 +112,26 @@
     order = sorted(range(1, size), key=lambda k: min(k, size - k))
     pending = []
 
+    def step_x(k, j, src, owner, group, by):
+        copy = remote(
+            src,
+            data_ref.at[owner, group],
+            x_send.at[k, j],
+            x_recv.at[k, j],
+            beside(lax.rem(x + by, wide)),
+        )
+        copy.start()
+        pending.append(copy)
+
     def forward(k, src, group):
-        for j in range(1, wide):
-            copy = remote(
-                src,
-                data_ref.at[x, group],
-                x_send.at[k, j],
-                x_recv.at[k, j],
-                beside(lax.rem(x + j, wide)),
-            )
-            copy.start()
-            pending.append(copy)
+        step_x(k, 1, src, x, group, 1)
+        step_x(k, 3, src, x, group, wide - 1)
+
+    def land_x(k, j, group):
+        origin = lax.rem(x + wide - j, wide)
+        landed = data_ref.at[origin, group]
+        remote(landed, landed, x_send.at[k, j], x_recv.at[k, j], beside(origin)).wait_recv()
+        return origin, landed
 
     for k in order:
         to = lax.rem(me + k, size)
@@ -146,14 +155,14 @@
         origin = lax.rem(me + size - k, size)
         landed = masks_ref.at[origin]
         remote(landed, landed, m_send.at[k], m_recv.at[k], peer(origin)).wait_recv()
+    for n, k in enumerate([0] + order):
+        group = lax.rem(me + size - k, size)
+        for j in (1, 3):
+            origin, landed = land_x(k, j, group)
+            if (j == 1) == (n % 4 in (0, 3)):
+                step_x(k, 2, landed, origin, group, j)
     for k in [0] + order:
-        group = lax.rem(me + size - k, size)
-        for j in range(1, wide):
-            origin = lax.rem(x + wide - j, wide)
-            landed = data_ref.at[origin, group]
-            remote(
-                landed, landed, x_send.at[k, j], x_recv.at[k, j], beside(origin)
-            ).wait_recv()
+        land_x(k, 2, lax.rem(me + size - k, size))
     for copy in pending:
         copy.wait_send()
     own.wait()
@@ -291,28 +300,39 @@
         remote(landed, landed, z_send.at[k], z_recv.at[k], along(origin)).wait_recv()
         forward(k, origin, landed_ref)
 
-    compute(0)
+    def offset(step):
+        return lax.rem(3 * step + 4, deep)
+
+    compute(offset(0))
     pl.semaphore_wait(barrier, count)
 
     @pl.loop(1, deep)
-    def _(k):
-        compute(k)
-
-        @pl.when(k == 1)
+    def _(step):
+        compute(offset(step))
+
+        @pl.when(step != 5)
+        def _():
+            send(offset(step - 1)).start()
+
+        @pl.when(step == 4)
+        def _():
+            receive(7)
+
+        @pl.when(step == 5)
         def _():
             forward(0, z, result_ref)
 
-        @pl.when(k >= 2)
+        @pl.when(step == 6)
         def _():
-            send(k - 1).start()
-
-        @pl.when(k >= 3)
+            receive(4)
+
+        @pl.when(step == 7)
         def _():
-            receive(k - 2)
-
-    send(deep - 1).start()
-    receive(deep - 2)
-    receive(deep - 1)
+            receive(2)
+
+    send(1).start()
+    for k in (5, 3, 6, 1):
+        receive(k)
     for k in range(deep):
         if k:
             send(k).wait_send()
@@ -345,6 +365,72 @@
         compiler_params=pltpu.CompilerParams(collective_id=2, has_side_effects=True),
         name="stack_pairs",
     )(index, mask, data)
+
+
+def lag_kernel(
+    stacked_ref, high_ref, low_ref, out_ref, part_ref, landed_ref, send_sem, recv_sem
+):
+    core, size, peer = place("core")
+    barrier, count = greet([(core, size, peer)])
+    stacked = stacked_ref[...]
+    high = stacked.astype(jnp.bfloat16)
+    low = (stacked - high.astype(jnp.float32)).astype(jnp.bfloat16)
+    chunks, rows, width = landed_ref.shape
+    other = 1 - core
+
+    def product(left, right):
+        return lax.dot_general(
+            left, right, (((0,), (0,)), ((), ())), preferred_element_type=jnp.float32
+        )
+
+    def copy(n):
+        return remote(
+            part_ref.at[n, pl.ds(pl.multiple_of(other * rows, rows), rows)],
+            landed_ref.at[n],
+            send_sem.at[n],
+            recv_sem.at[n],
+            peer(other),
+        )
+
+    for n in range(chunks):
+        lags = pl.ds(n * width, width)
+        part_ref[n] = (
+            product(high, high_ref[:, lags])
+            + product(high, low_ref[:, lags])
+            + product(low, high_ref[:, lags])
+        )
+        if n == 0:
+            pl.semaphore_wait(barrier, count)
+        else:
+            copy(n - 1).start()
+    copy(chunks - 1).start()
+    for n in range(chunks):
+        copy(n).wait_recv()
+        own = part_ref[n, pl.ds(pl.multiple_of(core * rows, rows), rows)]
+        out_ref[:, pl.ds(n * width, width)] = own + landed_ref[n]
+    for n in range(chunks):
+        copy(n).wait_send()
+
+
+def lag_product(stacked, high, low, chunks=4):
+    rows = stacked.shape[1] // 2
+    width = LAGS // chunks
+    vmem = pl.BlockSpec(memory_space=pltpu.VMEM)
+    dma = pltpu.SemaphoreType.DMA
+    return pl.pallas_call(
+        lag_kernel,
+        out_shape=jax.ShapeDtypeStruct((rows, LAGS), jnp.float32),
+        in_specs=[vmem] * 3,
+        out_specs=vmem,
+        scratch_shapes=[
+            pltpu.VMEM((chunks, 2 * rows, width), jnp.float32),
+            pltpu.VMEM((chunks, rows, width), jnp.float32),
+            dma((chunks,)),
+            dma((chunks,)),
+        ],
+        compiler_params=pltpu.CompilerParams(collective_id=3, has_side_effects=True),
+        name="lag_product",
+    )(stacked, high, low)
 
 
 def angles(bins, scale_bins):
@@ -386,7 +472,6 @@
             column,
             owner_code[None],
             listed.astype(jnp.int32)[None],
-            jnp.zeros((4, catalogue), jnp.int32),
         ]
     )
     blocks = spectra[0].reshape(stations, 2, NZ, bins // NZ).transpose(2, 0, 1, 3)
@@ -398,15 +483,10 @@
     data = data.reshape(NX, groups * 2 * f, NZ * stations)
     mask = mask.astype(jnp.float32).transpose(1, 0, 2)
     stacked = stack_pairs(index, mask, data, slots)
-    halves = lax.dot_general(
-        stacked.reshape(bins, slots // NY),
-        table,
-        (((0,), (0,)), ((), ())),
-        precision=lax.Precision.HIGH,
-        preferred_element_type=jnp.float32,
-    )
-    (halves,) = exchange("core", 3, ("swap", halves.reshape(2, slots // groups, LAGS)))
-    return halves[0] + halves[1]
+    high = lax.reduce_precision(table, exponent_bits=8, mantissa_bits=7)
+    low = (table - high).astype(jnp.bfloat16)
+    high = high.astype(jnp.bfloat16)
+    return lag_product(stacked.reshape(bins, slots // NY), high, low)
 
 
 def solution(mesh):

time: 116 us -> 105 us (0.905)
  Pallas kernels: 96.7 us -> 90.6 us
  matrix products: 4.34 us -> 0 us
    pallas_call x0 -> x1, Pallas kernels: none -> 8.71 us  [lag_product(): pl.pallas_call(lag_kernel, out_shape=jax.ShapeDtypeStruct((rows, LAGS), j...]
    pallas_call x2 -> x1, Pallas kernels: 26.8 us -> 19.6 us  [exchange(): pl.pallas_call(functools.partial(exchange_kernel, axis, modes), out_shape...]
    pallas_call x1, Pallas kernels: 41.1 us -> 34.3 us  [stack_pairs(): pl.pallas_call(stack_kernel, out_shape=jax.ShapeDtypeStruct((NY, NZ, rows...]
    dot_general x1 -> x0, matrix products: 4.34 us -> none  [local(): lax.dot_general(stacked.reshape(bins, slots // NY), table, (((0,), (0,)),...]
    convert_element_type x0 -> x1, other arithmetic: none -> 2.9 us  [local(): low = (table - high).astype(jnp.bfloat16)]
    another operation x1, other arithmetic: 2.25 us -> 0.31 us  [half_table(): return jnp.stack([real, imag], axis=2).reshape(bins, LAGS)]
    add x1 -> x0, other arithmetic: 1.76 us -> none  [local(): return halves[0] + halves[1]]
    unnamed x9 -> x10, local copies, waits for them, and re-layouts: 0.06 us -> 1.73 us
where the time goes in v3:
time: 105 us
  Pallas kernels  90.6 us (86%)
  other arithmetic  8.19 us (8%)
  local copies, waits for them, and re-layouts  5.99 us (6%)
    pallas_call x1, Pallas kernels, stack_pairs(): pl.pallas_call(stack_kernel, out_shape=jax.ShapeDtypeStruct((NY, NZ, rows...  34.3 us
    pallas_call x1, Pallas kernels, turn(): pl.pallas_call(turn_kernel, out_shape=[jax.ShapeDtypeStruct((NX,) + block...  28 us
    pallas_call x1, Pallas kernels, exchange(): pl.pallas_call(functools.partial(exchange_kernel, axis, modes), out_shape...  19.6 us
    pallas_call x1, Pallas kernels, lag_product(): pl.pallas_call(lag_kernel, out_shape=jax.ShapeDtypeStruct((rows, LAGS), j...  8.71 us
    convert_element_type x1, other arithmetic, local(): low = (table - high).astype(jnp.bfloat16)  2.9 us
    pallas_call x2, local copies, waits for them, and re-layouts, exchange(): pl.pallas_call(functools.partial(exchange_kernel, axis, modes), out_shape...  2.13 us

profile of v3, /device:TPU:1, one launch (start us, length us, event | category | flops | bytes accessed | tf_op | source)
XLA Modules:
  0.0 104.9 jit_solution(17316223473367953499)
XLA Ops:
  0.0 1.1 %fusion.6 = (f32[8,8,1024]{2,1,0:T(8,128)S(1)}, f32[8,8,1024]{2,1,0:T(8,128)S(1)}) fusion(s32[1024]{0:T(1024)S(1)} %iota_add_fusion, s32[8,8]{1,0:T(8,128)S(1)} %fusion.14), kind=kLoop, calls=%fused_computation.20 | loop fusion | flops 917504 | bytes 528640 | tf_op jit(solution)/shard_map/cos | solution.py:440
  1.1 0.2 cosine_multiply_fusion
  1.4 0.6 multiply_subtract_fusion
  2.0 0.3 pad_maximum_fusion
  2.3 0.0 copy-start
  2.3 0.0 copy-start.1
  2.3 0.0 copy-start.3
  2.3 0.0 copy-start.2
  2.3 2.9 %fusion = (bf16[1024,1024]{1,0:T(8,128)(2,1)}, bf16[1024,1024]{1,0:T(8,128)(2,1)}) fusion(f32[8,8,2,8,1024]{4,3,2,1,0:T(8,128)S(1)} %pad_maximum_fusion), kind=kLoop, calls=%fused_computation.2 | loop fusion | flops 4194304 | bytes 8388608 | tf_op jit(solution)/shard_map/convert_element_type | solution.py:487
  5.2 0.0 copy-done
  5.3 0.2 copy.23
  5.5 0.9 reshape.196.refs_0_
  6.3 0.0 copy-done.1
  6.4 0.0 copy-done.3
  6.4 0.2 fusion.1
  6.6 0.0 copy-done.2
  6.6 0.6 pad_add_fusion.refs_1_
  7.2 19.6 %exchange_z.1 = (bf16[8,64,256]{2,1,0:T(8,128)(2,1)}, s32[8,4,512]{2,1,0:T(4,128)}) custom-call(bf16[8,64,256]{2,1,0:T(8,128)(2,1)} %reshape.196.refs_0_, s32[4,512]{1,0:T(4,128)} %pad_add_fusion.refs_1_), custom_call_target="tpu_custom_call" | custom-call | tf_op jit(solution)/shard_map/exchange_z/pallas_call | solution.py:202
  26.8 0.9 copy.17
  27.6 0.6 fusion.10.mask_ref
  28.2 1.3 %copy.15 = bf16[8,64,256]{1,0,2:T(8,128)(2,1)S(1)} copy(bf16[8,64,256]{2,1,0:T(8,128)(2,1)} %get-tuple-element.10) | data formatting | bytes 524288 | tf_op jit(solution)/shard_map/exchange_z/pallas_call | solution.py:202
  29.5 0.3 reshape.197
  29.8 0.7 copy_bitcast_fusion.block_ref
  30.6 28.0 %turn.1 = (bf16[4,16,16,512]{3,2,1,0:T(8,128)(2,1)}, bf16[16,8,512]{2,1,0:T(8,128)(2,1)}) custom-call(bf16[16,16,512]{2,1,0:T(8,128)(2,1)} %copy_bitcast_fusion.block_ref, bf16[8,512]{1,0:T(8,128)(2,1)} %fusion.10.mask_ref), custom_call_target="tpu_custom_call" | custom-call | tf_op jit(solution)/shard_map/turn/pallas_call | solution.py:176
  58.6 1.7 %convert_bitcast_fusion.mask_ref = f32[8,16,512]{2,1,0:T(8,128)} fusion(bf16[16,8,512]{2,1,0:T(8,128)(2,1)} %get-tuple-element.11), kind=kLoop, calls=%fused_computation.18 | loop fusion | flops 65536 | bytes 393216 | tf_op jit(solution)/shard_map/transpose | solution.py:484
  60.2 34.3 %stack_pairs.1 = f32[8,8,16,128]{3,2,1,0:T(8,128)} custom-call(s32[8,4,512]{2,1,0:T(4,128)} %get-tuple-element.9.index_ref, f32[8,16,512]{2,1,0:T(8,128)} %convert_bitcast_fusion.mask_ref, bf16[4,256,512]{2,1,0:T(8,128)(2,1)} %bitcast.27), custom_call_target="tpu_custom_call" | custom-call | tf_op jit(solution)/shard_map/stack_pairs/pallas_call | solution.py:356
  94.5 8.7 %lag_product.1 = f32[64,1024]{1,0:T(8,128)} custom-call(f32[1024,128]{1,0:T(8,128)} %bitcast.26, bf16[1024,1024]{1,0:T(8,128)(2,1)} %get-tuple-element.14.high_ref, bf16[1024,1024]{1,0:T(8,128)(2,1)} %get-tuple-element.13.low_ref), custom_call_target="tpu_custom_call" | custom-call | tf_op jit(solution)/shard_map/lag_product/pallas_call | solution.py:420
  103.2 1.7 %copy.25 = f32[64,1024]{1,0:T(8,128)} copy(f32[64,1024]{1,0:T(8,128)} %lag_product.1) | data formatting | bytes 524288
  (6 shorter events, 0.1 us)
Async XLA Ops:
  2.3 2.9 %copy-start = (bf16[1,64,2048]{2,1,0:T(8,128)(2,1)S(1)}, bf16[1,64,2048]{2,1,0:T(8,128)(2,1)}, u32[]{:S(2)}) copy-start(bf16[1,64,2048]{2,1,0:T(8,128)(2,1)} %param.4) | copy-start | bytes 786436
  2.3 4.1 %copy-start.1 = (s32[2,512]{1,0:T(2,128)S(1)}, s32[2,512]{1,0:T(2,128)}, u32[]{:S(2)}) copy-start(s32[2,512]{1,0:T(2,128)} %param.6) | copy-start | bytes 12292
  2.3 4.1 %copy-start.3 = (s32[1,1,256]{2,1,0:T(1,128)S(1)}, s32[1,1,256]{2,1,0:T(1,128)}, u32[]{:S(2)}) copy-start(s32[1,1,256]{2,1,0:T(1,128)} %param.5) | copy-start | bytes 3076
  2.3 4.3 %copy-start.2 = (s32[512]{0:T(512)S(1)}, s32[512]{0:T(512)}, u32[]{:S(2)}) copy-start(s32[512]{0:T(512)} %param.7) | copy-start | bytes 6148

commit v4 on v3

--- a/solution.py
+++ b/solution.py
@@ -133,6 +133,14 @@
         remote(landed, landed, x_send.at[k, j], x_recv.at[k, j], beside(origin)).wait_recv()
         return origin, landed
 
+    def relay(n):
+        k = ([0] + order)[n]
+        group = lax.rem(me + size - k, size)
+        for j in (1, 3):
+            origin, landed = land_x(k, j, group)
+            if (j == 1) == (n % 4 in (0, 3)):
+                step_x(k, 2, landed, origin, group, j)
+
     for k in order:
         to = lax.rem(me + k, size)
         copy = remote(
@@ -146,21 +154,19 @@
         copy = remote(mask_ref, masks_ref.at[me], m_send.at[k], m_recv.at[k], peer(to))
         copy.start()
         pending.append(copy)
-    for k in order:
+    for n, k in enumerate(order):
         origin = lax.rem(me + size - k, size)
         landed = data_ref.at[x, origin]
         remote(landed, landed, t_send.at[k], t_recv.at[k], peer(origin)).wait_recv()
         forward(k, landed, origin)
+        if n >= 3:
+            relay(n - 3)
     for k in order:
         origin = lax.rem(me + size - k, size)
         landed = masks_ref.at[origin]
         remote(landed, landed, m_send.at[k], m_recv.at[k], peer(origin)).wait_recv()
-    for n, k in enumerate([0] + order):
-        group = lax.rem(me + size - k, size)
-        for j in (1, 3):
-            origin, landed = land_x(k, j, group)
-            if (j == 1) == (n % 4 in (0, 3)):
-                step_x(k, 2, landed, origin, group, j)
+    for n in range(size - 4, size):
+        relay(n)
     for k in [0] + order:
         land_x(k, 2, lax.rem(me + size - k, size))
     for copy in pending:
@@ -234,7 +240,7 @@
 
     a = pick(first)
     b = pick(second)
-    mask = mask_ref[c][:, None, :]
+    mask = mask_ref[:, pl.ds(c, 1), :]
     real = jnp.sum((a[:, 0] * b[:, 0] + a[:, 1] * b[:, 1]) * mask, axis=0)
     imag = jnp.sum((a[:, 0] * b[:, 1] - a[:, 1] * b[:, 0]) * mask, axis=0)
     value = jnp.concatenate([real, imag], axis=0)
@@ -251,7 +257,7 @@
 
 def stack_kernel(
     index_ref, mask_ref, data_ref, out_ref,
-    result_ref, landed_ref, z_send, z_recv, y_send, y_recv, own_sem,
+    result_ref, landed_ref, wide_ref, z_send, z_recv, y_send, y_recv, own_sem,
 ):
     z, deep, along = place("z")
     y, tall, above = place("y")
@@ -259,7 +265,7 @@
     barrier, count = greet([(z, deep, along), (y, tall, above)])
 
     def compute(k):
-        stack_one(index_ref, mask_ref, data_ref, result_ref, lax.rem(z + k, deep))
+        stack_one(index_ref, wide_ref, data_ref, result_ref, lax.rem(z + k, deep))
 
     def send(k):
         to = lax.rem(z + k, deep)
@@ -303,6 +309,7 @@
     def offset(step):
         return lax.rem(3 * step + 4, deep)
 
+    wide_ref[...] = mask_ref[...].astype(jnp.float32)
     compute(offset(0))
     pl.semaphore_wait(barrier, count)
 
@@ -359,6 +366,7 @@
         in_specs=[vmem] * 3,
         out_specs=vmem,
         scratch_shapes=[pltpu.VMEM((NZ, rows, slots), jnp.float32)] * 2
+        + [pltpu.VMEM(mask.shape, jnp.float32)]
         + [dma((NZ,))] * 2
         + [dma((NZ, NY))] * 2
         + [dma((NZ,))],
@@ -368,7 +376,8 @@
 
 
 def lag_kernel(
-    stacked_ref, high_ref, low_ref, out_ref, part_ref, landed_ref, send_sem, recv_sem
+    stacked_ref, cos_c_ref, sin_c_ref, cos_f_ref, sin_f_ref, out_ref,
+    part_ref, landed_ref, send_sem, recv_sem,
 ):
     core, size, peer = place("core")
     barrier, count = greet([(core, size, peer)])
@@ -394,10 +403,17 @@
 
     for n in range(chunks):
         lags = pl.ds(n * width, width)
+        cos_c, sin_c = cos_c_ref[:, lags][None, :, None], sin_c_ref[:, lags][None, :, None]
+        cos_f, sin_f = cos_f_ref[:, :, lags][:, None], sin_f_ref[:, :, lags][:, None]
+        real = cos_c * cos_f - sin_c * sin_f
+        imag = -(sin_c * cos_f + cos_c * sin_f)
+        table = jnp.stack([real, imag], axis=2).reshape(stacked.shape[0], width)
+        table_high = table.astype(jnp.bfloat16)
+        table_low = (table - table_high.astype(jnp.float32)).astype(jnp.bfloat16)
         part_ref[n] = (
-            product(high, high_ref[:, lags])
-            + product(high, low_ref[:, lags])
-            + product(low, high_ref[:, lags])
+            product(high, table_high)
+            + product(high, table_low)
+            + product(low, table_high)
         )
         if n == 0:
             pl.semaphore_wait(barrier, count)
@@ -412,7 +428,7 @@
         copy(n).wait_send()
 
 
-def lag_product(stacked, high, low, chunks=4):
+def lag_product(stacked, angles_of, chunks=4):
     rows = stacked.shape[1] // 2
     width = LAGS // chunks
     vmem = pl.BlockSpec(memory_space=pltpu.VMEM)
@@ -420,7 +436,7 @@
     return pl.pallas_call(
         lag_kernel,
         out_shape=jax.ShapeDtypeStruct((rows, LAGS), jnp.float32),
-        in_specs=[vmem] * 3,
+        in_specs=[vmem] * 5,
         out_specs=vmem,
         scratch_shapes=[
             pltpu.VMEM((chunks, 2 * rows, width), jnp.float32),
@@ -430,7 +446,7 @@
         ],
         compiler_params=pltpu.CompilerParams(collective_id=3, has_side_effects=True),
         name="lag_product",
-    )(stacked, high, low)
+    )(stacked, *angles_of)
 
 
 def angles(bins, scale_bins):
@@ -440,7 +456,7 @@
     return jnp.cos(phase), jnp.sin(phase)
 
 
-def half_table(bins):
+def half_angles(bins):
     core = lax.axis_index("tm") % 2
     coarse = jnp.arange(NZ, dtype=jnp.int32) * (bins // NZ)
     number = jnp.arange(NY * 8, dtype=jnp.int32)
@@ -448,11 +464,12 @@
     cos_c, sin_c = angles(coarse, bins)
     cos_f, sin_f = angles(fine, bins)
     scale = 1.0 / bins**0.5
-    cos_c, sin_c = (cos_c * scale)[None, :, None], (sin_c * scale)[None, :, None]
-    cos_f, sin_f = cos_f.reshape(NY, 1, 8, LAGS), sin_f.reshape(NY, 1, 8, LAGS)
-    real = cos_c * cos_f - sin_c * sin_f
-    imag = -(sin_c * cos_f + cos_c * sin_f)
-    return jnp.stack([real, imag], axis=2).reshape(bins, LAGS)
+    return (
+        cos_c * scale,
+        sin_c * scale,
+        cos_f.reshape(NY, 8, LAGS),
+        sin_f.reshape(NY, 8, LAGS),
+    )
 
 
 def local(spectra, pair_list, pair_stations, owner_code):
@@ -462,7 +479,7 @@
     groups = 2 * NY
     slots = 2 * catalogue
     f = bins // (NZ * groups)
-    table = half_table(bins)
+    angles_of = half_angles(bins)
     shard, inner = pair_stations // stations, pair_stations % stations
     column = (shard % NX) * (NZ * stations) + (shard // NX) * stations + inner
     number = jnp.arange(catalogue, dtype=jnp.int32)
@@ -481,12 +498,8 @@
     turned = blocks.reshape(NZ * stations, 2, groups, f).transpose(2, 1, 3, 0)
     data, mask = turn(turned.reshape(groups, 2 * f, NZ * stations), mask)
     data = data.reshape(NX, groups * 2 * f, NZ * stations)
-    mask = mask.astype(jnp.float32).transpose(1, 0, 2)
     stacked = stack_pairs(index, mask, data, slots)
-    high = lax.reduce_precision(table, exponent_bits=8, mantissa_bits=7)
-    low = (table - high).astype(jnp.bfloat16)
-    high = high.astype(jnp.bfloat16)
-    return lag_product(stacked.reshape(bins, slots // NY), high, low)
+    return lag_product(stacked.reshape(bins, slots // NY), angles_of)
 
 
 def solution(mesh):

time: 105 us -> 103 us (0.981)
  other arithmetic: 8.19 us -> 4.18 us
  local copies, waits for them, and re-layouts: 5.99 us -> 8.01 us
    convert_element_type x1 -> x0, other arithmetic: 2.9 us -> none  [local(): low = (table - high).astype(jnp.bfloat16)]
    unnamed x10, local copies, waits for them, and re-layouts: 1.73 us -> 4.6 us
    pallas_call x1, Pallas kernels: 34.3 us -> 31.7 us  [stack_pairs(): pl.pallas_call(stack_kernel, out_shape=jax.ShapeDtypeStruct((NY, NZ, rows...]
    sin x0 -> x1, other arithmetic: none -> 1.92 us  [angles(): return (jnp.cos(phase), jnp.sin(phase))]
    pallas_call x1, Pallas kernels: 8.71 us -> 10.6 us  [lag_product(): pl.pallas_call(lag_kernel, out_shape=jax.ShapeDtypeStruct((rows, LAGS), j...]
    transpose x1 -> x0, other arithmetic: 1.65 us -> none  [local(): mask = mask.astype(jnp.float32).transpose(1, 0, 2)]
    cos x1 -> x0, other arithmetic: 1.1 us -> none  [angles(): return (jnp.cos(phase), jnp.sin(phase))]
where the time goes in v4:
time: 103 us; the launch traced here: 102 us
  Pallas kernels  90.2 us (88%)
  local copies, waits for them, and re-layouts  8.01 us (8%)
  other arithmetic  4.18 us (4%)
    pallas_call x1, Pallas kernels, stack_pairs(): pl.pallas_call(stack_kernel, out_shape=jax.ShapeDtypeStruct((NY, NZ, rows...  31.7 us
    pallas_call x1, Pallas kernels, turn(): pl.pallas_call(turn_kernel, out_shape=[jax.ShapeDtypeStruct((NX,) + block...  28.3 us
    pallas_call x1, Pallas kernels, exchange(): pl.pallas_call(functools.partial(exchange_kernel, axis, modes), out_shape...  19.6 us
    pallas_call x1, Pallas kernels, lag_product(): pl.pallas_call(lag_kernel, out_shape=jax.ShapeDtypeStruct((rows, LAGS), j...  10.6 us
    unnamed x10, local copies, waits for them, and re-layouts  4.6 us

profile of v4, /device:TPU:1, one launch (start us, length us, event | category | flops | bytes accessed | tf_op | source)
XLA Modules:
  0.0 102.5 jit_solution(954689940873489712)
XLA Ops:
  0.0 1.0 copy.16
  1.0 0.2 copy.19
  1.2 0.9 reshape.84.refs_0_
  2.1 0.0 copy-start.3
  2.1 0.7 copy-done.3
  2.8 0.0 copy-start.1
  2.8 0.2 fusion
  2.9 0.5 copy-done.1
  3.4 0.0 copy-start.2
  3.5 0.6 copy-done.2
  4.1 0.6 pad_add_fusion.refs_1_
  4.7 19.6 %exchange_z.1 = (bf16[8,64,256]{2,1,0:T(8,128)(2,1)}, s32[8,4,512]{2,1,0:T(4,128)}) custom-call(bf16[8,64,256]{2,1,0:T(8,128)(2,1)} %reshape.84.refs_0_, s32[4,512]{1,0:T(4,128)} %pad_add_fusion.refs_1_), custom_call_target="tpu_custom_call" | custom-call | tf_op jit(solution)/shard_map/exchange_z/pallas_call | solution.py:208
  24.3 1.3 %copy.13 = bf16[8,64,256]{1,0,2:T(8,128)(2,1)S(1)} copy(bf16[8,64,256]{2,1,0:T(8,128)(2,1)} %get-tuple-element.10) | data formatting | bytes 524288 | tf_op jit(solution)/shard_map/exchange_z/pallas_call | solution.py:208
  25.6 0.3 reshape.85
  25.9 0.0 copy-start
  25.9 0.7 copy_bitcast_fusion.block_ref
  26.7 0.1 copy-done
  26.8 0.6 fusion.9.mask_ref
  27.4 28.3 %turn.1 = (bf16[4,16,16,512]{3,2,1,0:T(8,128)(2,1)}, bf16[16,8,512]{2,1,0:T(8,128)(2,1)}) custom-call(bf16[16,16,512]{2,1,0:T(8,128)(2,1)} %copy_bitcast_fusion.block_ref, bf16[8,512]{1,0:T(8,128)(2,1)} %fusion.9.mask_ref), custom_call_target="tpu_custom_call" | custom-call | tf_op jit(solution)/shard_map/turn/pallas_call | solution.py:182
  55.7 31.7 %stack_pairs.1 = f32[8,8,16,128]{3,2,1,0:T(8,128)} custom-call(s32[8,4,512]{2,1,0:T(4,128)} %get-tuple-element.9.index_ref, bf16[16,8,512]{2,1,0:T(8,128)(2,1)} %get-tuple-element.11.mask_ref, bf16[4,256,512]{2,1,0:T(8,128)(2,1)} %bitcast.22), custom_call_target="tpu_custom_call" | custom-call | tf_op jit(solution)/shard_map/stack_pairs/pallas_call | solution.py:363
  87.5 0.8 sine_multiply_fusion
  88.3 1.9 %fusion.4 = (f32[8,8,1024]{2,1,0:T(8,128)}, f32[8,8,1024]{2,1,0:T(8,128)}) fusion(s32[1024]{0:T(1024)S(1)} %iota_add_fusion, s32[8,8]{1,0:T(8,128)S(1)} %fusion.13), kind=kLoop, calls=%fused_computation.12 | loop fusion | flops 917504 | bytes 528640 | tf_op jit(solution)/shard_map/sin | solution.py:456
  90.2 10.6 %lag_product.1 = f32[64,1024]{1,0:T(8,128)} custom-call(f32[1024,128]{1,0:T(8,128)} %bitcast.21, f32[8,1024]{1,0:T(8,128)} %get-tuple-element.16.cos_c_ref, f32[8,1024]{1,0:T(8,128)} %get-tuple-element.15.sin_c_ref, f32[8,8,1024]{2,1,0:T(8,128)} %get-tuple-element.14.cos_f_ref, f32[8,8,1024]{2,1,0:T(8,128)} %get-tuple-element.13.sin_f_ref), custom_call_target="tpu_custom_call" | custom-call | tf_op jit(solution)/shard_map/lag_product/pallas_call | solution.py:436
  100.8 1.7 %copy.21 = f32[64,1024]{1,0:T(8,128)} copy(f32[64,1024]{1,0:T(8,128)} %lag_product.1) | data formatting | bytes 524288
  (6 shorter events, 0.1 us)
Async XLA Ops:
  2.1 0.7 copy-start.3
  2.8 0.7 copy-start.1
  3.4 0.7 copy-start.2
  25.9 0.8 copy-start
